TPU v7x, 32 devices: a whole 2x2x4 slice. The times are simulated.
32 devices in a mesh: ctx: 8 (over z, y), pack: 4 (over x, core).
Axes of the slice: x: 2, y: 2, z: 4, core: 2. Of those that a mesh axis runs over, the one named last changes fastest.
Arguments:
- hidden: bfloat16 [8192, 2048], P(('ctx', 'pack')), may hold values from -4 to 4
- first_keys: bfloat16 [8192, 2048], P('ctx', 'pack'), may hold values from -400 to 400
- first_values: bfloat16 [8192, 2048], P('ctx', 'pack'), may hold values from -18 to 18
- w_query: bfloat16 [2048, 2048], P(None, 'pack'), may hold values from -0.125 to 0.125
- w_out: bfloat16 [2048, 2048], P('pack'), may hold values from -0.125 to 0.125
- norm_gain: float32 [2048], replicated, may hold values from 0.1 to 1.9
- router_weight: float32 [2048], replicated, may hold values from -0.5 to 0.5
- route_list: int32 [8, 256], P('ctx'), may hold values from 0 to 1023, as said below
- pack_order: int32 [8, 256], P('ctx'), may hold values from 0 to 255, each once within a row
- pattern: int32 [8, 12], replicated, may hold values from 0 to 7
Outputs:
- hidden_out: bfloat16 [8192, 2048], P(('ctx', 'pack'))
- packed_states: bfloat16 [2048, 2048], P(('ctx', 'pack'))
Inputs may be any that keep to these rules, and one draw needn't show every extreme that they name: `route_list`: each row lists 256 distinct span-local positions in ascending order. At most 96 of a row's positions lie among the 256 tokens of one device, and in every row some device holds exactly 96.
All inputs are finite; a program needn't handle non-finite values.
Results may differ from a plain program's by a relative error of at most 0.023.
Values may be sent and summed in bfloat16 or wider, within the bound.
No kernel may reach another device: no remote copies, remote signals or barrier semaphores. Data moves between devices by JAX's collectives and lax.ppermute only.
A program may use at most 128 MiB of HBM per device.

v0:
```python
import math
import jax
import jax.numpy as jnp
from jax import lax
from jax.sharding import PartitionSpec as P

HD = 128
epsilon = 1e-06
very_negative = -1e30


def rotate(projected, position, head_count):
    row_count = projected.shape[0]
    head_size = projected.shape[1] // head_count
    half_size = head_size // 2
    frequency = 10000.0 ** (-jnp.arange(half_size, dtype=jnp.float32) * 2.0 / head_size)
    angle = position.astype(jnp.float32)[:, None] * frequency[None, :]
    cosine = jnp.cos(angle)[:, None, :]
    sine_part = jnp.sin(angle)[:, None, :]
    shaped = projected.reshape(row_count, head_count, head_size)
    front_half = shaped[..., :half_size]
    back_half = shaped[..., half_size:]
    turned = jnp.concatenate(
        [front_half * cosine - back_half * sine_part, back_half * cosine + front_half * sine_part],
        axis=-1,
    )
    return turned.reshape(row_count, head_count * head_size)


def partial_block(query_heads, key_heads, value_heads, allowed):
    scale_factor = 1.0 / math.sqrt(query_heads.shape[2])
    scores = (
        jnp.einsum("qhd,khd->hqk", query_heads, key_heads, preferred_element_type=jnp.float32)
        * scale_factor
    )
    if allowed is not None:
        scores = jnp.where(allowed[None], scores, very_negative)
    row_peak = jnp.max(scores, axis=-1)
    weights = jnp.exp(scores - row_peak[..., None])
    if allowed is not None:
        weights = jnp.where(allowed[None], weights, 0.0)
    weight_sum = jnp.sum(weights, axis=-1)
    rounded = weights.astype(jnp.bfloat16)
    summed = jnp.einsum("hqk,khd->qhd", rounded, value_heads, preferred_element_type=jnp.float32)
    return (row_peak, weight_sum, summed)


def merge(former, latter):
    new_peak = jnp.maximum(former[0], latter[0])
    former_scale = jnp.exp(former[0] - new_peak)
    latter_scale = jnp.exp(latter[0] - new_peak)
    weight_sum = former_scale * former[1] + latter_scale * latter[1]
    summed = (
        jnp.transpose(former_scale)[:, :, None] * former[2]
        + jnp.transpose(latter_scale)[:, :, None] * latter[2]
    )
    return (new_peak, weight_sum, summed)


def local(
    hidden,
    first_keys,
    first_values,
    w_query,
    w_out,
    norm_gain,
    router_weight,
    route_list,
    pack_order,
    pattern,
):
    n_pack = lax.axis_size("pack")
    span_id = lax.axis_index("ctx")
    pack_id = lax.axis_index("pack")
    tok_dev = hidden.shape[0]
    model_width = hidden.shape[1]
    span_len = tok_dev * n_pack
    routes = route_list[0]
    slot_order = pack_order[0]
    routed = routes.shape[0]
    per_slot = routed // n_pack
    capacity = 3 * tok_dev // 8
    local_width = first_keys.shape[1]
    head_count = local_width // HD
    lane_ids = jnp.arange(n_pack, dtype=jnp.int32)
    starts = jnp.sum((routes[None, :] < (lane_ids * tok_dev)[:, None]).astype(jnp.int32), axis=1)
    run_ends = jnp.concatenate([starts[1:], jnp.full((1,), routed, jnp.int32)])
    my_start = jnp.sum(jnp.where(lane_ids == pack_id, starts, 0))
    my_count = jnp.sum(jnp.where(lane_ids == pack_id, run_ends - starts, 0))
    padded = jnp.concatenate([routes, jnp.full((capacity,), span_len, jnp.int32)])
    sending = lax.dynamic_slice_in_dim(padded, my_start, capacity, 0)
    is_valid = jnp.arange(capacity, dtype=jnp.int32) < my_count
    local_rows = jnp.clip(sending - pack_id * tok_dev, 0, tok_dev - 1)
    outgoing = jnp.where(is_valid[:, None], hidden[local_rows], jnp.zeros((), hidden.dtype))
    gathered = lax.all_gather(outgoing, "pack", axis=0, tiled=True)
    picked = routes[slot_order]
    owner_id = picked // tok_dev
    owner_start = jnp.sum(
        jnp.where(owner_id[:, None] == lane_ids[None, :], starts[None, :], 0), axis=1
    )
    source_row = owner_id * capacity + (slot_order - owner_start)
    routed_rows = gathered[source_row]
    position = span_id * span_len + picked
    rows_float = routed_rows.astype(jnp.float32)
    mean_square = jnp.mean(rows_float * rows_float, axis=-1, keepdims=True)
    normed = (rows_float * lax.rsqrt(mean_square + epsilon) * norm_gain).astype(jnp.bfloat16)
    queries = rotate(
        jnp.dot(normed, w_query, preferred_element_type=jnp.float32), position, head_count
    ).astype(jnp.bfloat16)
    query_heads = queries.reshape(routed, head_count, HD)
    key_heads = first_keys.reshape(span_len, head_count, HD)
    value_heads = first_values.reshape(span_len, head_count, HD)
    key_pos = span_id * span_len + jnp.arange(span_len, dtype=jnp.int32)
    own_state = partial_block(
        query_heads, key_heads, value_heads, key_pos[None, :] <= position[:, None]
    )
    wanted = pattern[span_id]
    running = own_state
    key_piece = lax.all_gather(first_keys, "ctx", axis=0, tiled=True)
    value_piece = lax.all_gather(first_values, "ctx", axis=0, tiled=True)
    blocks = key_piece.shape[0] // span_len
    key_stack = key_piece.reshape(blocks, span_len, head_count, HD)
    value_stack = value_piece.reshape(blocks, span_len, head_count, HD)

    def visit(held, block_item):
        block_idx, key_block, value_block = block_item
        active = jnp.logical_and(block_idx < span_id, jnp.any(wanted == block_idx))
        held = lax.cond(
            active,
            lambda inner: merge(inner, partial_block(query_heads, key_block, value_block, None)),
            lambda inner: inner,
            held,
        )
        return (held, None)

    running, unused = lax.scan(
        visit, running, (jnp.arange(blocks, dtype=jnp.int32), key_stack, value_stack)
    )
    attended = (
        (running[2] / jnp.transpose(running[1])[:, :, None])
        .reshape(routed, local_width)
        .astype(jnp.bfloat16)
    )
    mixed = lax.psum_scatter(
        jnp.dot(attended, w_out, preferred_element_type=jnp.float32),
        "pack",
        scatter_dimension=0,
        tiled=True,
    )
    own_rows = lax.dynamic_slice_in_dim(rows_float, pack_id * per_slot, per_slot, 0)
    gate_value = jax.nn.sigmoid(jnp.dot(own_rows, router_weight, precision=lax.Precision.HIGHEST))
    packed_states = (own_rows + gate_value[:, None] * mixed).astype(jnp.bfloat16)
    target = jnp.where(is_valid, sending - pack_id * tok_dev, tok_dev)
    slot_rows = lax.dynamic_slice_in_dim(source_row, pack_id * per_slot, per_slot, 0)
    returning = (
        jnp.zeros((n_pack * capacity, model_width), jnp.float32)
        .at[slot_rows]
        .set(packed_states.astype(jnp.float32))
    )
    arrived = lax.psum_scatter(
        returning.astype(jnp.bfloat16), "pack", scatter_dimension=0, tiled=True
    )
    hidden_out = hidden.at[target].set(arrived, mode="drop")
    return (hidden_out, packed_states)


def solution(mesh):
    return jax.shard_map(
        local,
        mesh=mesh,
        in_specs=(
            P(("ctx", "pack"), None),
            P("ctx", "pack"),
            P("ctx", "pack"),
            P(None, "pack"),
            P("pack", None),
            P(),
            P(),
            P("ctx", None),
            P("ctx", None),
            P(),
        ),
        out_specs=(P(("ctx", "pack"), None), P(("ctx", "pack"), None)),
        check_vma=False,
    )
```

profile of v0, /device:TPU:0, one launch (start us, length us, event | category | flops | bytes accessed | tf_op | source)
XLA Modules:
  0.0 461.3 jit_solution(13582422450582323742)
XLA Ops:
  7.2 1.4 copy.80
  8.6 0.9 convert_reduce_fusion
  9.5 0.1 slice.9
  9.5 0.7 fusion.55
  11.6 1.2 iota_compare_fusion.1
  13.4 2.0 compare_select_fusion.2
  15.4 0.8 gather_fusion.1
  16.3 1.5 broadcast_select_fusion
  17.8 0.0 all-gather.6.cloned.1.call-start
  17.9 0.7 all-gather.6.cloned.1.call-update
  18.6 0.7 all-gather.8.cloned.1.call-update
  19.4 1.9 gather_fusion
  21.4 0.7 fusion.54
  22.1 0.1 select_reduce_fusion
  22.2 0.5 multiply_cosine_fusion
  22.7 0.9 broadcast_compare_fusion
  23.7 16.7 %all-gather.4.cloned.1.call-done = bf16[384,2048]{1,0:T(8,128)(2,1)} async-done(((bf16[96,2048]{1,0:T(8,128)(2,1)}), bf16[384,2048]{1,0:T(8,128)(2,1)}) %all-gather.4.cloned.1.call-update) | async-done | bytes 1572880 | tf_op jit(solution)/shard_map/all_gather | solution.py:95
  40.3 4.9 %gather_fusion.2 = bf16[256,2048]{1,0:T(8,128)(2,1)} fusion(bf16[384,2048]{1,0:T(8,128)(2,1)} %all-gather.4.cloned.1.call-done, s32[1024]{0:T(1024)S(1)} %pad_clamp_fusion), kind=kCustom, calls=%fused_computation.2 | custom fusion | bytes 2098176 | tf_op jit(solution)/shard_map/gather | solution.py:102
  45.3 1.5 multiply_reduce_fusion
  46.8 3.5 fusion.41
  50.3 2.1 reshape.245
  52.4 1.6 fusion.62
  54.0 0.1 subtract_convert_fusion
  54.2 0.1 pad_maximum_fusion
  54.3 2.0 fusion.26
  56.4 1.5 fusion.28
  57.9 2.3 fusion.34
  60.2 106.8 %all-gather.6.cloned.1.call-done = bf16[8192,512]{1,0:T(8,128)(2,1)} async-done(((bf16[1024,512]{1,0:T(8,128)(2,1)}), bf16[8192,512]{1,0:T(8,128)(2,1)}) %all-gather.6.cloned.1.call-update) | async-done | bytes 8388624 | tf_op jit(solution)/shard_map/all_gather | solution.py:119
  167.0 12.7 %reshape.295 = bf16[8,1024,4,128]{3,2,1,0:T(4,128)(2,1)} reshape(bf16[8192,512]{1,0:T(8,128)(2,1)} %all-gather.6.cloned.1.call-done) | data formatting | bytes 16777216 | tf_op jit(solution)/shard_map/reshape | solution.py:122
  179.7 8.7 %copy.34 = bf16[8,1024,4,128]{3,1,2,0:T(8,128)(2,1)} copy(bf16[8,1024,4,128]{3,2,1,0:T(4,128)(2,1)} %reshape.295) | data formatting | bytes 16777216 | tf_op jit(solution)/shard_map/while | solution.py:136
  188.4 103.4 %all-gather.8.cloned.1.call-done = bf16[8192,512]{1,0:T(8,128)(2,1)} async-done(((bf16[1024,512]{1,0:T(8,128)(2,1)}), bf16[8192,512]{1,0:T(8,128)(2,1)}) %all-gather.8.cloned.1.call-update) | async-done | bytes 8388624 | tf_op jit(solution)/shard_map/all_gather | solution.py:120
  291.8 12.5 %reshape.296 = bf16[8,1024,4,128]{3,2,1,0:T(4,128)(2,1)} reshape(bf16[8192,512]{1,0:T(8,128)(2,1)} %all-gather.8.cloned.1.call-done) | data formatting | bytes 16777216 | tf_op jit(solution)/shard_map/reshape | solution.py:123
  304.3 8.7 %copy.35 = bf16[8,1024,4,128]{3,1,2,0:T(8,128)(2,1)} copy(bf16[8,1024,4,128]{3,2,1,0:T(4,128)(2,1)} %reshape.296) | data formatting | bytes 16777216 | tf_op jit(solution)/shard_map/while | solution.py:136
  313.0 25.6 %while.14 = (s32[]{:T(128)}, f32[4,256]{1,0:T(4,128)S(1)}, f32[4,256]{1,0:T(4,128)S(1)}, f32[256,4,128]{2,0,1:T(8,128)}, s32[8]{0:T(128)S(1)}, /*index=5*/s32[]{...) while((s32[]{:T(128)}, f32[4,256]{1,0:T(4,128)S(1)}, ...), condition=%wide.region_13.14_spmd, body=%wide.region_7.13_spmd.sunk | while | flops 545657856 | bytes 20264304 | solution.py:136
  313.0 0.6 dynamic_slice.65
  314.3 1.3 compare_reduce_fusion.2
  316.2 0.6 dynamic_slice.65
  317.5 1.3 compare_reduce_fusion.2
  319.4 0.6 dynamic_slice.65
  320.7 1.3 compare_reduce_fusion.2
  322.6 0.6 dynamic_slice.65
  323.9 1.3 compare_reduce_fusion.2
  325.8 0.6 dynamic_slice.65
  327.1 1.3 compare_reduce_fusion.2
  329.0 0.6 dynamic_slice.65
  330.3 1.3 compare_reduce_fusion.2
  332.2 0.6 dynamic_slice.65
  333.5 1.3 compare_reduce_fusion.2
  335.4 0.6 dynamic_slice.65
  336.7 1.3 compare_reduce_fusion.2
  338.6 2.0 copy.36
  340.6 1.1 divide_convert_fusion
  341.7 2.1 fusion.63
  343.8 0.0 reduce-scatter.5.cloned.1.call-start
  343.9 0.1 compare_select_fusion.3
  344.0 2.8 convert_element_type.45
  346.8 1.3 fusion.40
  348.0 68.0 %reduce-scatter.3.cloned.1.call-done = f32[64,2048]{1,0:T(8,128)} async-done(((f32[256,2048]{1,0:T(8,128)}), f32[64,2048]{1,0:T(8,128)}) %reduce-scatter.3.cloned.1.call-update) | async-done | bytes 524304 | tf_op jit(solution)/shard_map/reduce_scatter | solution.py:144
  416.0 1.3 add_convert_fusion
  417.4 2.8 scatter_custom_fusion
  420.1 3.3 convert_element_type.53
  423.4 28.1 %reduce-scatter.5.cloned.1.call-done = bf16[96,2048]{1,0:T(8,128)(2,1)} async-done(((bf16[384,2048]{1,0:T(8,128)(2,1)}), bf16[96,2048]{1,0:T(8,128)(2,1)}) %reduce-scatter.5.cloned.1.call-update) | async-done | bytes 393232 | tf_op jit(solution)/shard_map/reduce_scatter | solution.py:160
  451.6 2.2 scatter_fusion
  453.8 1.0 copy-done.2
  (47 shorter events, 0.4 us)
Async XLA Ops:
  7.2 334.6 %copy-start = (bf16[512,2048]{1,0:T(8,128)(2,1)S(1)}, bf16[512,2048]{1,0:T(8,128)(2,1)}, u32[]{:S(2)}) copy-start(bf16[512,2048]{1,0:T(8,128)(2,1)} %param.18) | copy-start | bytes 6291460
  7.2 12.2 %copy-start.1 = (s32[1,256]{1,0:T(1,128)S(1)}, s32[1,256]{1,0:T(1,128)}, u32[]{:S(2)}) copy-start(s32[1,256]{1,0:T(1,128)} %param.21) | copy-start | bytes 3076
  7.2 12.2 %copy-start.9 = (s32[1,256]{1,0:T(1,128)S(1)}, s32[1,256]{1,0:T(1,128)}, u32[]{:S(2)}) copy-start(s32[1,256]{1,0:T(1,128)} %param.22) | copy-start | bytes 3076
  7.2 33.1 %all-gather.4.cloned.1.call-start = ((), (), s32[]{:S(2)}) async-start(), calls=%async_computation.2 | async-start | bytes 1966080 | tf_op jit(solution)/shard_map/all_gather | solution.py:95
  17.8 149.1 %all-gather.6.cloned.1.call-start = ((), (), s32[]{:S(2)}) async-start(), calls=%async_computation.3 | async-start | bytes 9437184 | tf_op jit(solution)/shard_map/all_gather | solution.py:119
  18.6 273.2 %all-gather.8.cloned.1.call-start = ((), (), s32[]{:S(2)}) async-start(), calls=%async_computation.4 | async-start | bytes 9437184 | tf_op jit(solution)/shard_map/all_gather | solution.py:120
  19.3 396.7 %reduce-scatter.3.cloned.1.call-start = ((), (), s32[]{:S(2)}) async-start(), calls=%async_computation.5 | async-start | bytes 2621440 | tf_op jit(solution)/shard_map/reduce_scatter | solution.py:144
  23.7 23.1 %copy-start.12 = (f32[2048]{0:T(1024)S(1)}, f32[2048]{0:T(1024)}, u32[]{:S(2)}) copy-start(f32[2048]{0:T(1024)} %param.19) | copy-start | bytes 24580
  52.4 2.0 copy-start.5
  54.0 2.4 copy-start.6
  54.3 3.6 copy-start.7
  341.7 5.0 %copy-start.10 = (f32[2048]{0:T(1024)S(1)}, f32[2048]{0:T(1024)}, u32[]{:S(2)}) copy-start(f32[2048]{0:T(1024)} %param.20) | copy-start | bytes 24580
  343.8 107.7 %reduce-scatter.5.cloned.1.call-start = ((), (), s32[]{:S(2)}) async-start(), calls=%async_computation.6 | async-start | bytes 1966080 | tf_op jit(solution)/shard_map/reduce_scatter | solution.py:160
  417.3 6.1 %copy-start.8 = (bf16[64,2048]{1,0:T(8,128)(2,1)}, bf16[64,2048]{1,0:T(8,128)(2,1)S(1)}, u32[]{:S(2)}) copy-start(bf16[64,2048]{1,0:T(8,128)(2,1)S(1)} %add_convert_fusion) | copy-start | bytes 786436
  417.4 34.2 %copy-start.11 = (s32[96]{0:T(128)S(1)}, s32[96]{0:T(128)}, u32[]{:S(2)}) copy-start(s32[96]{0:T(128)} %get-tuple-element.184) | copy-start | bytes 1156
  453.8 1.0 copy-start.2
Sparse Core Ops, SparseCore 0:
  17.9 22.3 all-gather.3
  42.5 124.4 all-gather.5
  169.1 122.6 all-gather.7
  344.0 72.0 reduce-scatter.2
  423.5 27.9 reduce-scatter.4
where the time goes:
time: 463 us; the launch traced here: 461 us
  waiting for transfers between devices  324 us (70%)
  local copies, waits for them, and re-layouts  66.4 us (14%)
  other arithmetic  32.7 us (7%)
  between operations  16 us (3%)
  matrix products  11.1 us (2%)
  loops' own time  10.5 us (2%)
    all_gather x1, waiting for transfers between devices, local(): key_piece = lax.all_gather(first_keys, 'ctx', axis=0, tiled=True)  107 us
    all_gather x1, waiting for transfers between devices, local(): value_piece = lax.all_gather(first_values, 'ctx', axis=0, tiled=True)  103 us
    reduce_scatter x1, waiting for transfers between devices, local(): lax.psum_scatter(jnp.dot(attended, w_out, preferred_element_type=jnp.floa...  68 us
    reduce_scatter x1, waiting for transfers between devices, local(): lax.psum_scatter(returning.astype(jnp.bfloat16), 'pack', scatter_dimensio...  28.1 us
    while x3, local copies, waits for them, and re-layouts, local(): lax.scan(visit, running, (jnp.arange(blocks, dtype=jnp.int32), key_stack,...  19.4 us
    all_gather x1, waiting for transfers between devices, local(): gathered = lax.all_gather(outgoing, 'pack', axis=0, tiled=True)  16.7 us
    reshape x1, local copies, waits for them, and re-layouts, local(): key_stack = key_piece.reshape(blocks, span_len, head_count, HD)  12.7 us
    reshape x1, local copies, waits for them, and re-layouts, local(): value_stack = value_piece.reshape(blocks, span_len, head_count, HD)  12.5 us
  transfers between devices with their start and end apart: 5, of which 5 were waited for; matrix products, arithmetic and copies ran while one was open for 11% of the time, Pallas kernels for 0%

commit v1 on v0

--- a/solution.py
+++ b/solution.py
@@ -116,7 +116,19 @@
     )
     wanted = pattern[span_id]
     running = own_state
-    key_piece = lax.all_gather(first_keys, "ctx", axis=0, tiled=True)
+    q_n = lax.axis_size("ctx")
+    runs = tuple(((i, (i + 1) % q_n) for i in range(q_n)))
+    found = tuple(((i, (i - 1) % q_n) for i in range(q_n)))
+    before, item_now = ([first_keys], [first_keys])
+    for _ in range(q_n // 2):
+        y2 = lax.ppermute(before[-1], "ctx", runs)
+        before.append(y2)
+    for _ in range((q_n - 1) // 2):
+        carry_out = lax.ppermute(item_now[-1], axis_name="ctx", perm=found)
+        item_now.append(carry_out)
+    val2 = jnp.concatenate([*before[::-1], *item_now[1:]], axis=0)
+    mat_out = lax.axis_index("ctx")
+    key_piece = jnp.roll(val2, (mat_out - q_n // 2) * first_keys.shape[0], axis=0)
     value_piece = lax.all_gather(first_values, "ctx", axis=0, tiled=True)
     blocks = key_piece.shape[0] // span_len
     key_stack = key_piece.reshape(blocks, span_len, head_count, HD)

time: 463 us -> 473 us (1.022)
  waiting for transfers between devices: 324 us -> 276 us
  local copies, waits for them, and re-layouts: 66.4 us -> 105 us
  starting transfers between devices: 0.2 us -> 19 us
    ppermute x0 -> x7, waiting for transfers between devices: none -> 175 us  [the longest x4 174 us: local(): y2 = lax.ppermute(before[-1], 'ctx', runs)]
    all_gather x1 -> x0, waiting for transfers between devices: 107 us -> none  [local(): key_piece = lax.all_gather(first_keys, 'ctx', axis=0, tiled=True)]
    all_gather x1, waiting for transfers between devices: 103 us -> 0.01 us  [local(): value_piece = lax.all_gather(first_values, 'ctx', axis=0, tiled=True)]
    unnamed x23 -> x40, local copies, waits for them, and re-layouts: 2.38 us -> 31.9 us
    ppermute x0 -> x7, starting transfers between devices: none -> 18.7 us  [the longest x4 10.5 us: local(): y2 = lax.ppermute(before[-1], 'ctx', runs)]
    all_gather x1, waiting for transfers between devices: 16.7 us -> 0.01 us  [local(): gathered = lax.all_gather(outgoing, 'pack', axis=0, tiled=True)]
    dynamic_slice x0 -> x1, local copies, waits for them, and re-layouts: none -> 7.14 us  [local(): jnp.roll(val2, (mat_out - q_n // 2) * first_keys.shape[0], axis=0)]
  transfers between devices with their start and end apart: 5 -> 11, of which waited for: 5 -> 7; matrix products, arithmetic and copies ran while one was open for 11% -> 19% of each run, Pallas kernels for 0% -> 0%
where the time goes in v1:
time: 473 us; the launch traced here: 470 us
  waiting for transfers between devices  276 us (58%)
  local copies, waits for them, and re-layouts  105 us (22%)
  other arithmetic  33.7 us (7%)
  starting transfers between devices  19 us (4%)
  between operations  16 us (3%)
  matrix products  11 us (2%)
  loops' own time  9.89 us (2%)
    ppermute x4, waiting for transfers between devices, local(): y2 = lax.ppermute(before[-1], 'ctx', runs)  174 us
    reduce_scatter x1, waiting for transfers between devices, local(): lax.psum_scatter(jnp.dot(attended, w_out, preferred_element_type=jnp.floa...  71.4 us
    unnamed x40, local copies, waits for them, and re-layouts  31.9 us
    reduce_scatter x1, waiting for transfers between devices, local(): lax.psum_scatter(returning.astype(jnp.bfloat16), 'pack', scatter_dimensio...  28.2 us
    while x3, local copies, waits for them, and re-layouts, local(): lax.scan(visit, running, (jnp.arange(blocks, dtype=jnp.int32), key_stack,...  19.4 us
    reshape x1, local copies, waits for them, and re-layouts, local(): value_stack = value_piece.reshape(blocks, span_len, head_count, HD)  12.5 us
    reshape x1, local copies, waits for them, and re-layouts, local(): key_stack = key_piece.reshape(blocks, span_len, head_count, HD)  12.5 us
    ppermute x4, starting transfers between devices, local(): y2 = lax.ppermute(before[-1], 'ctx', runs)  10.5 us
  transfers between devices with their start and end apart: 11, of which 7 were waited for; matrix products, arithmetic and copies ran while one was open for 19% of the time, Pallas kernels for 0%

profile of v1, /device:TPU:0, one launch (start us, length us, event | category | flops | bytes accessed | tf_op | source)
XLA Modules:
  0.0 470.2 jit_solution(17724178534697085532)
XLA Ops:
  7.2 1.4 copy.95
  12.2 1.2 iota_compare_fusion.1
  14.1 2.0 compare_select_fusion.2
  16.9 1.5 broadcast_select_fusion
  19.2 3.0 collective-permute-start
  22.2 3.1 collective-permute-start.4
  25.3 1.9 gather_fusion
  27.3 51.3 %collective-permute-done = bf16[1024,512]{1,0:T(8,128)(2,1)} collective-permute-done((bf16[1024,512]{1,0:T(8,128)(2,1)}, bf16[1024,512]{1,0:T(8,128)(2,1)}, u32[]{:S(2)}, u32[]{:S(2)}) %collective-permute-start) | collective-permute-done | bytes 1048608 | tf_op jit(solution)/shard_map/ppermute | solution.py:124
  78.7 2.5 collective-permute-start.1
  81.2 3.0 collective-permute-start.5
  87.1 46.2 %collective-permute-done.1 = bf16[1024,512]{1,0:T(8,128)(2,1)} collective-permute-done((bf16[1024,512]{1,0:T(8,128)(2,1)}, bf16[1024,512]{1,0:T(8,128)(2,1)}, u32[]{:S(2)}, u32[]{:S(2)}) %collective-permute-start.1) | collective-permute-done | bytes 1048608 | tf_op jit(solution)/shard_map/ppermute | solution.py:124
  133.4 2.5 collective-permute-start.2
  135.9 1.0 collective-permute-done.5
  136.9 2.0 collective-permute-start.6
  138.9 4.9 %gather_fusion.2 = bf16[256,2048]{1,0:T(8,128)(2,1)} fusion(bf16[384,2048]{1,0:T(8,128)(2,1)} %all-gather.3.cloned.1.call-done, s32[1024]{0:T(1024)S(1)} %pad_clamp_fusion), kind=kCustom, calls=%fused_computation.2 | custom fusion | bytes 2098176 | tf_op jit(solution)/shard_map/gather | solution.py:102
  143.9 1.5 multiply_reduce_fusion
  145.4 3.5 fusion.41
  148.9 2.0 reshape.245
  150.9 1.6 fusion.62
  152.9 50.2 %collective-permute-done.2 = bf16[1024,512]{1,0:T(8,128)(2,1)} collective-permute-done((bf16[1024,512]{1,0:T(8,128)(2,1)}, bf16[1024,512]{1,0:T(8,128)(2,1)}, u32[]{:S(2)}, u32[]{:S(2)}) %collective-permute-start.2) | collective-permute-done | bytes 1048608 | tf_op jit(solution)/shard_map/ppermute | solution.py:124
  203.1 2.5 collective-permute-start.3
  205.5 2.0 fusion.26
  207.5 2.2 fusion.34
  209.8 1.5 fusion.28
  211.3 26.6 %collective-permute-done.3 = bf16[1024,512]{1,0:T(8,128)(2,1)S(1)} collective-permute-done((bf16[1024,512]{1,0:T(8,128)(2,1)}, bf16[1024,512]{1,0:T(8,128)(2,1)S(1)}, u32[]{:S(2)}, u32[]{:S(2)}) %collective-permute-start.3) | collective-permute-done | bytes 1048608 | tf_op jit(solution)/shard_map/ppermute | solution.py:124
  238.9 2.3 constant_dynamic-update-slice_fusion.14
  241.2 2.4 constant_dynamic-update-slice_fusion.13
  243.6 2.3 constant_dynamic-update-slice_fusion.12
  246.9 2.3 constant_dynamic-update-slice_fusion.10
  249.2 2.3 constant_dynamic-update-slice_fusion.9
  251.5 2.3 constant_dynamic-update-slice_fusion.8
  253.8 1.1 constant_dynamic-update-slice_fusion.7
  254.9 2.2 constant_dynamic-update-slice_fusion.6
  257.2 2.3 constant_dynamic-update-slice_fusion.5
  259.4 2.3 constant_dynamic-update-slice_fusion.4
  261.7 1.1 constant_dynamic-update-slice_fusion.3
  262.8 2.3 constant_dynamic-update-slice_fusion.2
  265.1 2.3 constant_dynamic-update-slice_fusion.1
  267.4 2.3 constant_dynamic-update-slice_fusion
  269.6 7.1 %constant_dynamic-slice_fusion = bf16[8192,512]{1,0:T(8,128)(2,1)} fusion(bf16[16384,512]{1,0:T(8,128)(2,1)} %constant_dynamic-update-slice_fusion, s32[]{:T(128)S(6)} %select_n.113), kind=kLoop, calls=%fused_computation.110 | loop fusion | bytes 16777220 | tf_op jit(solution)/shard_map/jit(_roll_dynamic)/dynamic_slice | solution.py:131
  276.8 12.5 %reshape.295 = bf16[8,1024,4,128]{3,2,1,0:T(4,128)(2,1)} reshape(bf16[8192,512]{1,0:T(8,128)(2,1)} %constant_dynamic-slice_fusion) | data formatting | bytes 16777216 | tf_op jit(solution)/shard_map/reshape | solution.py:134
  289.3 8.7 %copy.34 = bf16[8,1024,4,128]{3,1,2,0:T(8,128)(2,1)} copy(bf16[8,1024,4,128]{3,2,1,0:T(4,128)(2,1)} %reshape.295) | data formatting | bytes 16777216 | tf_op jit(solution)/shard_map/while | solution.py:148
  298.0 12.5 %reshape.296 = bf16[8,1024,4,128]{3,2,1,0:T(4,128)(2,1)} reshape(bf16[8192,512]{1,0:T(8,128)(2,1)} %all-gather.5.cloned.1.call-done) | data formatting | bytes 16777216 | tf_op jit(solution)/shard_map/reshape | solution.py:135
  310.6 8.7 %copy.35 = bf16[8,1024,4,128]{3,1,2,0:T(8,128)(2,1)} copy(bf16[8,1024,4,128]{3,2,1,0:T(4,128)(2,1)} %reshape.296) | data formatting | bytes 16777216 | tf_op jit(solution)/shard_map/while | solution.py:148
  319.2 24.6 %while.14 = (s32[]{:T(128)}, f32[4,256]{1,0:T(4,128)S(1)}, f32[4,256]{1,0:T(4,128)S(1)}, f32[256,4,128]{2,0,1:T(8,128)}, s32[8]{0:T(128)S(1)}, /*index=5*/s32[]{...) while((s32[]{:T(128)}, f32[4,256]{1,0:T(4,128)S(1)}, ...), condition=%wide.region_13.14_spmd, body=%wide.region_7.13_spmd.sunk | while | flops 545657856 | bytes 20264296 | solution.py:148
  319.8 1.2 compare_reduce_fusion.2
  322.9 1.2 compare_reduce_fusion.2
  326.0 1.2 compare_reduce_fusion.2
  329.0 1.2 compare_reduce_fusion.2
  332.1 1.2 compare_reduce_fusion.2
  335.2 1.2 compare_reduce_fusion.2
  338.3 1.2 compare_reduce_fusion.2
  341.3 1.2 compare_reduce_fusion.2
  343.8 2.0 copy.36
  345.9 1.1 divide_convert_fusion
  347.0 2.1 fusion.63
  349.4 2.8 convert_element_type.45
  352.2 1.3 fusion.40
  353.5 71.4 %reduce-scatter.3.cloned.1.call-done = f32[64,2048]{1,0:T(8,128)} async-done(((f32[256,2048]{1,0:T(8,128)}), f32[64,2048]{1,0:T(8,128)}) %reduce-scatter.3.cloned.1.call-update) | async-done | bytes 524304 | tf_op jit(solution)/shard_map/reduce_scatter | solution.py:156
  424.8 1.3 add_convert_fusion
  426.2 2.7 scatter_custom_fusion
  428.9 3.3 convert_element_type.53
  432.2 28.2 %reduce-scatter.5.cloned.1.call-done = bf16[96,2048]{1,0:T(8,128)(2,1)} async-done(((bf16[384,2048]{1,0:T(8,128)(2,1)}), bf16[96,2048]{1,0:T(8,128)(2,1)}) %reduce-scatter.5.cloned.1.call-update) | async-done | bytes 393232 | tf_op jit(solution)/shard_map/reduce_scatter | solution.py:172
  460.4 2.2 scatter_fusion
  (76 shorter events, 15.5 us)
Async XLA Ops:
  7.2 339.8 %copy-start = (bf16[512,2048]{1,0:T(8,128)(2,1)S(1)}, bf16[512,2048]{1,0:T(8,128)(2,1)}, u32[]{:S(2)}) copy-start(bf16[512,2048]{1,0:T(8,128)(2,1)} %param.18) | copy-start | bytes 6291460
  7.2 18.2 %copy-start.1 = (s32[1,256]{1,0:T(1,128)S(1)}, s32[1,256]{1,0:T(1,128)}, u32[]{:S(2)}) copy-start(s32[1,256]{1,0:T(1,128)} %param.21) | copy-start | bytes 3076
  7.2 78.5 %copy-start.9 = (s32[1,256]{1,0:T(1,128)S(1)}, s32[1,256]{1,0:T(1,128)}, u32[]{:S(2)}) copy-start(s32[1,256]{1,0:T(1,128)} %param.22) | copy-start | bytes 3076
  7.2 131.7 %all-gather.3.cloned.1.call-start = ((), (), s32[]{:S(2)}) async-start(), calls=%async_computation.2 | async-start | bytes 1966080 | tf_op jit(solution)/shard_map/all_gather | solution.py:95
  9.5 6.6 %copy-start.11 = (s32[4]{0:T(128)}, s32[4]{0:T(128)S(1)}, u32[]{:S(2)}) copy-start(s32[4]{0:T(128)S(1)} %convert_reduce_fusion) | copy-start | bytes 52
  18.4 279.6 %all-gather.5.cloned.1.call-start = ((), (), s32[]{:S(2)}) async-start(), calls=%async_computation.3 | async-start | bytes 9437184 | tf_op jit(solution)/shard_map/all_gather | solution.py:132
  19.1 405.7 %reduce-scatter.3.cloned.1.call-start = ((), (), s32[]{:S(2)}) async-start(), calls=%async_computation.4 | async-start | bytes 2621440 | tf_op jit(solution)/shard_map/reduce_scatter | solution.py:156
  19.2 59.5 %collective-permute-start = (bf16[1024,512]{1,0:T(8,128)(2,1)}, bf16[1024,512]{1,0:T(8,128)(2,1)}, u32[]{:S(2)}, u32[]{:S(2)}) collective-permute-start(bf16[1024,512]{1,0:T(8,128)(2,1)} %param.15), channel_id=1, source_target_pairs={{0,4},{4,8},{8,12},{12,16},{16,20},{20,24},{24,28},{28,0},{1,5},{5... | collective-permute-start | bytes 3145736 | tf_op jit(solution)/shard_map/ppermute | solution.py:124
  22.2 58.9 %collective-permute-start.4 = (bf16[1024,512]{1,0:T(8,128)(2,1)}, bf16[1024,512]{1,0:T(8,128)(2,1)}, u32[]{:S(2)}, u32[]{:S(2)}) collective-permute-start(bf16[1024,512]{1,0:T(8,128)(2,1)} %param.15), channel_id=1, source_target_pairs={{0,28},{4,0},{8,4},{12,8},{16,12},{20,16},{24,20},{28,24},{1,29},{... | collective-permute-start | bytes 3145736 | tf_op jit(solution)/shard_map/ppermute | solution.py:127
  78.7 54.7 %collective-permute-start.1 = (bf16[1024,512]{1,0:T(8,128)(2,1)}, bf16[1024,512]{1,0:T(8,128)(2,1)}, u32[]{:S(2)}, u32[]{:S(2)}) collective-permute-start(bf16[1024,512]{1,0:T(8,128)(2,1)} %collective-permute-done), channel_id=1, source_target_pairs={{0,4},{4,8},{8,12},{12,16},{16,20},{20,24},{24,28},{28,0},{1,5},{5... | collective-permute-start | bytes 3145736 | tf_op jit(solution)/shard_map/ppermute | solution.py:124
  81.2 55.8 %collective-permute-start.5 = (bf16[1024,512]{1,0:T(8,128)(2,1)}, bf16[1024,512]{1,0:T(8,128)(2,1)}, u32[]{:S(2)}, u32[]{:S(2)}) collective-permute-start(bf16[1024,512]{1,0:T(8,128)(2,1)} %collective-permute-done.4), channel_id=1, source_target_pairs={{0,28},{4,0},{8,4},{12,8},{16,12},{20,16},{24,20},{28,24},{1,29},{... | collective-permute-start | bytes 3145736 | tf_op jit(solution)/shard_map/ppermute | solution.py:127
  87.1 58.3 %copy-start.13 = (f32[2048]{0:T(1024)S(1)}, f32[2048]{0:T(1024)}, u32[]{:S(2)}) copy-start(f32[2048]{0:T(1024)} %param.19) | copy-start | bytes 24580
  133.4 69.7 %collective-permute-start.2 = (bf16[1024,512]{1,0:T(8,128)(2,1)}, bf16[1024,512]{1,0:T(8,128)(2,1)}, u32[]{:S(2)}, u32[]{:S(2)}) collective-permute-start(bf16[1024,512]{1,0:T(8,128)(2,1)} %collective-permute-done.1), channel_id=1, source_target_pairs={{0,4},{4,8},{8,12},{12,16},{16,20},{20,24},{24,28},{28,0},{1,5},{5... | collective-permute-start | bytes 3145736 | tf_op jit(solution)/shard_map/ppermute | solution.py:124
  136.9 114.6 %collective-permute-start.6 = (bf16[1024,512]{1,0:T(8,128)(2,1)}, bf16[1024,512]{1,0:T(8,128)(2,1)}, u32[]{:S(2)}, u32[]{:S(2)}) collective-permute-start(bf16[1024,512]{1,0:T(8,128)(2,1)} %collective-permute-done.5), channel_id=1, source_target_pairs={{0,28},{4,0},{8,4},{12,8},{16,12},{20,16},{24,20},{28,24},{1,29},{... | collective-permute-start | bytes 3145736 | tf_op jit(solution)/shard_map/ppermute | solution.py:127
  150.9 54.6 %copy-start.5 = (bf16[1024,512]{1,0:T(8,128)(2,1)S(1)}, bf16[1024,512]{1,0:T(8,128)(2,1)}, u32[]{:S(2)}) copy-start(bf16[1024,512]{1,0:T(8,128)(2,1)} %param.15) | copy-start | bytes 3145732
  152.5 55.0 %copy-start.6 = (pred[256,1024]{1,0:T(8,128)(4,1)S(1)}, pred[256,1024]{1,0:T(8,128)(4,1)}, u32[]{:S(2)}) copy-start(pred[256,1024]{1,0:T(8,128)(4,1)} %broadcast_compare_fusion) | copy-start | bytes 786436
  152.5 55.0 %copy-start.7 = (bf16[1024,512]{1,0:T(8,128)(2,1)S(1)}, bf16[1024,512]{1,0:T(8,128)(2,1)}, u32[]{:S(2)}) copy-start(bf16[1024,512]{1,0:T(8,128)(2,1)} %param.16) | copy-start | bytes 3145732
  203.1 34.8 %collective-permute-start.3 = (bf16[1024,512]{1,0:T(8,128)(2,1)}, bf16[1024,512]{1,0:T(8,128)(2,1)S(1)}, u32[]{:S(2)}, u32[]{:S(2)}) collective-permute-start(bf16[1024,512]{1,0:T(8,128)(2,1)} %collective-permute-done.2), channel_id=1, source_target_pairs={{0,4},{4,8},{8,12},{12,16},{16,20},{20,24},{24,28},{28,0},{1,5},{5... | collective-permute-start | bytes 3145736 | tf_op jit(solution)/shard_map/ppermute | solution.py:124
  347.0 5.3 %copy-start.10 = (f32[2048]{0:T(1024)S(1)}, f32[2048]{0:T(1024)}, u32[]{:S(2)}) copy-start(f32[2048]{0:T(1024)} %param.20) | copy-start | bytes 24580
  349.1 111.4 %reduce-scatter.5.cloned.1.call-start = ((), (), s32[]{:S(2)}) async-start(), calls=%async_computation.5 | async-start | bytes 1966080 | tf_op jit(solution)/shard_map/reduce_scatter | solution.py:172
  426.1 6.1 %copy-start.8 = (bf16[64,2048]{1,0:T(8,128)(2,1)}, bf16[64,2048]{1,0:T(8,128)(2,1)S(1)}, u32[]{:S(2)}) copy-start(bf16[64,2048]{1,0:T(8,128)(2,1)S(1)} %add_convert_fusion) | copy-start | bytes 786436
  426.2 34.3 %copy-start.12 = (s32[96]{0:T(128)S(1)}, s32[96]{0:T(128)}, u32[]{:S(2)}) copy-start(s32[96]{0:T(128)} %get-tuple-element.184) | copy-start | bytes 1156
  462.6 1.0 copy-start.2
Sparse Core Ops, SparseCore 0:
  18.5 22.3 all-gather.2
  43.0 224.1 all-gather.4
  349.2 75.6 reduce-scatter.2
  432.3 28.0 reduce-scatter.4
